TPU v7x, 512 devices: a whole 4x8x8 slice. The times are simulated.
512 devices in a mesh: space: 32 (over y, z_hi), tensor: 16 (over x, z_lo, core).
Axes of the slice: x: 4, y: 8, z: 8 (z_hi: 4, z_lo: 2; z = z_hi * 2 + z_lo), core: 2. Of those that a mesh axis runs over, the one named last changes fastest.
Arguments:
- features: bfloat16 [128, 128, 1024], P('space', None, 'tensor'), may hold values from -6 to 6
- depth_kernel: bfloat16 [2, 7, 7, 1024], P(None, None, None, 'tensor'), may hold values from -5 to 5
- norm_gain: float32 [2, 1024], replicated, may hold values from 0.5 to 1.5
- norm_bias: float32 [2, 1024], replicated, may hold values from -3 to 3
- w_expand: bfloat16 [2, 1024, 4096], P(None, None, 'tensor'), may hold values from -0.1875 to 0.1875
- b_expand: float32 [2, 4096], P(None, 'tensor'), may hold values from -3 to 3
- w_reduce: bfloat16 [2, 4096, 1024], P(None, 'tensor'), may hold values from -0.125 to 0.125
- b_reduce: float32 [2, 1024], P(None, 'tensor'), may hold values from -3 to 3
- layer_scale: float32 [2, 1024], P(None, 'tensor'), may hold values from 0.5 to 1.5
Outputs:
- output: bfloat16 [128, 128, 1024], P('space', None, 'tensor')
All inputs are finite; a program needn't handle non-finite values.
Results may differ from a plain program's by a relative error of at most 0.023.
Values may be sent and summed in bfloat16 or wider, within the bound.
No kernel may reach another device: no remote copies, remote signals or barrier semaphores. Data moves between devices by JAX's collectives and lax.ppermute only.
A program may use at most 64 MiB of HBM per device.

v0:
```python
import jax
import jax.numpy as jnp
from jax import lax
from jax.sharding import PartitionSpec as P

D = 1024
TAPS = 7
BLOCKS = 2


def with_halo(x, sides, width):
    for axis, dim in sides:
        devices, length = (lax.axis_size(axis), x.shape[dim])
        up = [(i, (i + 1) % devices) for i in range(devices - 1)]
        down = [(j, i) for i, j in up]
        last = lax.slice_in_dim(x, length - width, length, axis=dim)
        leading = lax.slice_in_dim(x, 0, width, axis=dim)
        before = lax.ppermute(last, axis, up)
        after = lax.ppermute(leading, axis, down)
        x = jnp.concatenate([before, x, after], axis=dim)
    return x


def one_block(stream, kernel, gain, bias, expand, bias_expand, reduce_w, bias_reduce, scale):
    half = TAPS // 2
    height, width, share = stream.shape
    positions = height * width
    padded = with_halo(stream, (("space", 0),), half)
    padded = jnp.pad(padded.astype(jnp.float32), ((0, 0), (half, half), (0, 0)))
    filtered = jnp.zeros(stream.shape, jnp.float32)
    for row_tap in range(TAPS):
        for col_tap in range(TAPS):
            filtered = filtered + padded[
                row_tap : row_tap + height, col_tap : col_tap + width
            ] * kernel[row_tap, col_tap].astype(jnp.float32)
    filtered = filtered.reshape(positions, share)
    offset = lax.axis_index("tensor") * share
    gain_part = lax.dynamic_slice_in_dim(gain, offset, share, 0)
    bias_part = lax.dynamic_slice_in_dim(bias, offset, share, 0)
    sums, squares = lax.psum(
        (jnp.sum(filtered, axis=-1), jnp.sum(filtered * filtered, axis=-1)), "tensor"
    )
    mean = (sums / D)[:, None]
    var = jnp.maximum(squares[:, None] / D - mean * mean, 0.0)
    normed_part = ((filtered - mean) / jnp.sqrt(var + 1e-06) * gain_part + bias_part).astype(
        jnp.bfloat16
    )
    preact = jnp.dot(
        lax.all_gather(normed_part, "tensor", axis=1, tiled=True),
        expand,
        preferred_element_type=jnp.float32,
    )
    hidden = jax.nn.gelu(preact + bias_expand, approximate=False).astype(jnp.bfloat16)
    partial_value = jnp.dot(hidden, reduce_w, preferred_element_type=jnp.float32)
    mixed = lax.psum_scatter(
        partial_value.astype(jnp.bfloat16), "tensor", scatter_dimension=1, tiled=True
    ).astype(jnp.float32)
    updated = stream.reshape(positions, share).astype(jnp.float32) + scale * (mixed + bias_reduce)
    return updated.astype(jnp.bfloat16).reshape(height, width, share)


def per_device(
    features,
    depth_kernel,
    norm_gain,
    norm_bias,
    w_expand,
    b_expand,
    w_reduce,
    b_reduce,
    layer_scale,
):
    stream = features
    for block_id in range(BLOCKS):
        stream = one_block(
            stream,
            depth_kernel[block_id],
            norm_gain[block_id],
            norm_bias[block_id],
            w_expand[block_id],
            b_expand[block_id],
            w_reduce[block_id],
            b_reduce[block_id],
            layer_scale[block_id],
        )
    return stream


def solution(mesh):
    return jax.shard_map(
        per_device,
        mesh=mesh,
        in_specs=(
            P("space", None, "tensor"),
            P(None, None, None, "tensor"),
            P(),
            P(),
            P(None, None, "tensor"),
            P(None, "tensor"),
            P(None, "tensor", None),
            P(None, "tensor"),
            P(None, "tensor"),
        ),
        out_specs=P("space", None, "tensor"),
        check_vma=False,
    )
```

profile of v0, /device:TPU:8, one launch (start us, length us, event | category | flops | bytes accessed | tf_op | source)
XLA Modules:
  0.0 327.0 jit_solution(3460924509859641475)
XLA Ops:
  6.5 0.9 fusion.455
  7.4 6.1 %collective-permute-start = (bf16[3,128,64]{1,2,0:T(8,128)(2,1)S(1)}, bf16[3,128,64]{1,2,0:T(8,128)(2,1)S(1)}, u32[]{:S(2)}, u32[]{:S(2)}) collective-permute-start(bf16[3,128,64]{1,2,0:T(8,128)(2,1)S(1)} %get-tuple-element.17), channel_id=1, source_target_pairs={{0,16},{16,32},{32,48},{48,64},{64,80},{80,96},{96,112},{112,128},... | collective-permute-start | bytes 147464 | tf_op jit(solution)/shard_map/ppermute | solution.py:18
  13.5 6.7 %collective-permute-start.1 = (bf16[3,128,64]{1,2,0:T(8,128)(2,1)S(1)}, bf16[3,128,64]{1,2,0:T(8,128)(2,1)S(1)}, u32[]{:S(2)}, u32[]{:S(2)}) collective-permute-start(bf16[3,128,64]{1,2,0:T(8,128)(2,1)S(1)} %get-tuple-element.18), channel_id=1, source_target_pairs={{16,0},{32,16},{48,32},{64,48},{80,64},{96,80},{112,96},{128,112},... | collective-permute-start | bytes 147464 | tf_op jit(solution)/shard_map/ppermute | solution.py:19
  20.2 0.9 fusion.456
  21.1 0.8 fusion.457
  21.9 0.8 fusion.458
  23.3 1.0 maximum_convert_fusion.1
  24.3 2.2 fusion.451
  26.5 29.5 %all-reduce.3 = (f32[512]{0:T(512)S(1)}, f32[512]{0:T(512)S(1)}) all-reduce(f32[512]{0:T(512)S(1)} %bitcast.584, f32[512]{0:T(512)S(1)} %bitcast.583), channel_id=1, replica_groups=mesh['space'=32,'tensor'=16] {'tensor'}, use_global_device_ids=true, to_apply=%region_3.4 | all-reduce | flops 1024 | bytes 8192 | tf_op jit(solution)/shard_map/psum | solution.py:40
  56.0 0.7 fusion.285
  56.8 35.1 %all-gather.3.cloned.1.call-done = bf16[512,1024]{0,1:T(8,128)(2,1)} async-done(((bf16[512,64]{0,1:T(8,128)(2,1)}), bf16[512,1024]{0,1:T(8,128)(2,1)}) %all-gather.3.cloned.1.call-update) | async-done | bytes 1048592 | tf_op jit(solution)/shard_map/all_gather | solution.py:49
  91.8 4.6 %convolution_convert_fusion.1 = bf16[512,1024]{0,1:T(8,128)(2,1)} fusion(bf16[2,256,1024]{2,1,0:T(8,128)(2,1)S(1)} %copy-done.4, bf16[512,1024]{0,1:T(8,128)(2,1)} %all-gather.3.cloned.1.call-done, bf16[2,1024,256]{2,1,0:T(8,128)(2,1)S(1)} %copy-done.5, f32[256]{0:T(256)S(1)} %bitcast.588), kind=kOutput, calls=%fused_computation.85 | convolution fusion | flops 546045952 | bytes 3146752 | tf_op jit(solution)/shard_map/dot_general | solution.py:54
  97.2 66.4 %reduce-scatter.3.cloned.1.call-done = bf16[512,64]{0,1:T(8,128)(2,1)} async-done(((bf16[512,1024]{0,1:T(8,128)(2,1)}), bf16[512,64]{0,1:T(8,128)(2,1)}) %reduce-scatter.3.cloned.1.call-update) | async-done | bytes 65552 | tf_op jit(solution)/shard_map/reduce_scatter | solution.py:55
  163.6 0.9 fusion.284
  164.6 5.5 %collective-permute-start.3 = (bf16[3,128,64]{1,0,2:T(4,128)(2,1)S(1)}, bf16[3,128,64]{1,0,2:T(4,128)(2,1)S(1)}, u32[]{:S(2)}, u32[]{:S(2)}) collective-permute-start(bf16[3,128,64]{1,0,2:T(4,128)(2,1)S(1)} %slice.780), channel_id=1, source_target_pairs={{16,0},{32,16},{48,32},{64,48},{80,64},{96,80},{112,96},{128,112},... | collective-permute-start | bytes 147464 | tf_op jit(solution)/shard_map/ppermute | solution.py:19
  170.1 1.9 collective-permute-start.2
  172.2 7.1 %collective-permute-done.2 = bf16[3,128,64]{1,0,2:T(4,128)(2,1)S(1)} collective-permute-done((bf16[3,128,64]{1,0,2:T(4,128)(2,1)S(1)}, bf16[3,128,64]{1,0,2:T(4,128)(2,1)S(1)}, u32[]{:S(2)}, u32[]{:S(2)}) %collective-permute-start.2) | collective-permute-done | bytes 49184 | tf_op jit(solution)/shard_map/ppermute | solution.py:18
  179.4 7.0 %fusion.450 = (f32[4,128]{1,0:T(4,128)S(1)}, f32[4,128]{1,0:T(4,128)S(1)}, f32[4,128,64]{1,0,2:T(4,128)S(1)}) fusion(f32[64]{0:T(128)S(1)} %get-tuple-element.22, f32[64]{0:T(128)S(1)} %get-tuple-element.23, f32[64]{0:T(128)S(1)} %get-tuple-element.24, f32[64]{0:T(128)S(1)} %get-tuple-element.25, f32[10,128,64]{1,0,2:T(8,128)S(1)} %maximum_convert_fusion, ...), kind=kLoop, calls=%fused_computation.684 | loop fusion | flops 3275776 | bytes 1602048 | tf_op jit(solution)/shard_map/reduce_sum | solution.py:41
  186.5 27.1 %all-reduce.2 = (f32[512]{0:T(512)S(1)}, f32[512]{0:T(512)S(1)}) all-reduce(f32[512]{0:T(512)S(1)} %bitcast.586, f32[512]{0:T(512)S(1)} %bitcast.585), channel_id=1, replica_groups=mesh['space'=32,'tensor'=16] {'tensor'}, use_global_device_ids=true, to_apply=%region_8.9 | all-reduce | flops 1024 | bytes 8192 | tf_op jit(solution)/shard_map/psum | solution.py:40
  213.6 0.7 fusion.286
  214.4 32.7 %all-gather.5.cloned.1.call-done = bf16[512,1024]{0,1:T(8,128)(2,1)} async-done(((bf16[512,64]{0,1:T(8,128)(2,1)}), bf16[512,1024]{0,1:T(8,128)(2,1)}) %all-gather.5.cloned.1.call-update) | async-done | bytes 1048592 | tf_op jit(solution)/shard_map/all_gather | solution.py:49
  247.1 4.6 %convolution_convert_fusion = bf16[512,1024]{0,1:T(8,128)(2,1)} fusion(bf16[2,256,1024]{2,1,0:T(8,128)(2,1)S(1)} %copy-done.4, bf16[512,1024]{0,1:T(8,128)(2,1)} %all-gather.5.cloned.1.call-done, bf16[2,1024,256]{2,1,0:T(8,128)(2,1)S(1)} %copy-done.5, f32[256]{0:T(256)S(1)} %bitcast.587), kind=kOutput, calls=%fused_computation.84 | convolution fusion | flops 546045952 | bytes 3146752 | tf_op jit(solution)/shard_map/dot_general | solution.py:54
  251.8 67.2 %reduce-scatter.5.cloned.1.call-done = bf16[512,64]{0,1:T(8,128)(2,1)} async-done(((bf16[512,1024]{0,1:T(8,128)(2,1)}), bf16[512,64]{0,1:T(8,128)(2,1)}) %reduce-scatter.5.cloned.1.call-update) | async-done | bytes 65552 | tf_op jit(solution)/shard_map/reduce_scatter | solution.py:55
  318.9 1.6 copy_bitcast_fusion
  (41 shorter events, 1.8 us)
Async XLA Ops:
  6.5 85.3 %all-gather.3.cloned.1.call-start = ((), (), s32[]{:S(2)}) async-start(), calls=%async_computation.2 | async-start | bytes 1114112 | tf_op jit(solution)/shard_map/all_gather | solution.py:49
  7.4 15.4 %collective-permute-start = (bf16[3,128,64]{1,2,0:T(8,128)(2,1)S(1)}, bf16[3,128,64]{1,2,0:T(8,128)(2,1)S(1)}, u32[]{:S(2)}, u32[]{:S(2)}) collective-permute-start(bf16[3,128,64]{1,2,0:T(8,128)(2,1)S(1)} %get-tuple-element.17), channel_id=1, source_target_pairs={{0,16},{16,32},{32,48},{48,64},{64,80},{80,96},{96,112},{112,128},... | collective-permute-start | bytes 147464 | tf_op jit(solution)/shard_map/ppermute | solution.py:18
  13.5 9.8 %collective-permute-start.1 = (bf16[3,128,64]{1,2,0:T(8,128)(2,1)S(1)}, bf16[3,128,64]{1,2,0:T(8,128)(2,1)S(1)}, u32[]{:S(2)}, u32[]{:S(2)}) collective-permute-start(bf16[3,128,64]{1,2,0:T(8,128)(2,1)S(1)} %get-tuple-element.18), channel_id=1, source_target_pairs={{16,0},{32,16},{48,32},{64,48},{80,64},{96,80},{112,96},{128,112},... | collective-permute-start | bytes 147464 | tf_op jit(solution)/shard_map/ppermute | solution.py:19
  22.8 34.0 %copy-start.1 = (f32[2,256]{1,0:T(2,128)S(1)}, f32[2,256]{1,0:T(2,128)}, u32[]{:S(2)}) copy-start(f32[2,256]{1,0:T(2,128)} %param.14) | copy-start | bytes 6148
  22.8 69.1 %copy-start.4 = (bf16[2,256,1024]{2,1,0:T(8,128)(2,1)S(1)}, bf16[2,256,1024]{2,1,0:T(8,128)(2,1)}, u32[]{:S(2)}) copy-start(bf16[2,256,1024]{2,1,0:T(8,128)(2,1)} %param.15) | copy-start | bytes 3145732
  22.8 69.1 %copy-start.5 = (bf16[2,1024,256]{2,1,0:T(8,128)(2,1)S(1)}, bf16[2,1024,256]{2,1,0:T(8,128)(2,1)}, u32[]{:S(2)}) copy-start(bf16[2,1024,256]{2,1,0:T(8,128)(2,1)} %param.13) | copy-start | bytes 3145732
  56.7 106.9 %reduce-scatter.3.cloned.1.call-start = ((), (), s32[]{:S(2)}) async-start(), calls=%async_computation.3 | async-start | bytes 1114112 | tf_op jit(solution)/shard_map/reduce_scatter | solution.py:55
  96.4 0.7 copy-start.2
  96.4 0.7 copy-start.3
  96.4 67.2 %copy-start = (bf16[4,128,64]{1,2,0:T(8,128)(2,1)S(1)}, bf16[4,128,64]{1,2,0:T(8,128)(2,1)}, u32[]{:S(2)}) copy-start(bf16[4,128,64]{1,2,0:T(8,128)(2,1)} %param.9) | copy-start | bytes 196612
  96.5 150.7 %all-gather.5.cloned.1.call-start = ((), (), s32[]{:S(2)}) async-start(), calls=%async_computation.4 | async-start | bytes 1114112 | tf_op jit(solution)/shard_map/all_gather | solution.py:49
  164.6 7.5 %collective-permute-start.3 = (bf16[3,128,64]{1,0,2:T(4,128)(2,1)S(1)}, bf16[3,128,64]{1,0,2:T(4,128)(2,1)S(1)}, u32[]{:S(2)}, u32[]{:S(2)}) collective-permute-start(bf16[3,128,64]{1,0,2:T(4,128)(2,1)S(1)} %slice.780), channel_id=1, source_target_pairs={{16,0},{32,16},{48,32},{64,48},{80,64},{96,80},{112,96},{128,112},... | collective-permute-start | bytes 147464 | tf_op jit(solution)/shard_map/ppermute | solution.py:19
  170.1 9.2 %collective-permute-start.2 = (bf16[3,128,64]{1,0,2:T(4,128)(2,1)S(1)}, bf16[3,128,64]{1,0,2:T(4,128)(2,1)S(1)}, u32[]{:S(2)}, u32[]{:S(2)}) collective-permute-start(bf16[3,128,64]{1,0,2:T(4,128)(2,1)S(1)} %slice.778), channel_id=1, source_target_pairs={{0,16},{16,32},{32,48},{48,64},{64,80},{80,96},{96,112},{112,128},... | collective-permute-start | bytes 147464 | tf_op jit(solution)/shard_map/ppermute | solution.py:18
  214.4 104.6 %reduce-scatter.5.cloned.1.call-start = ((), (), s32[]{:S(2)}) async-start(), calls=%async_computation.5 | async-start | bytes 1114112 | tf_op jit(solution)/shard_map/reduce_scatter | solution.py:55
Sparse Core Ops, SparseCore 0:
  56.8 34.9 all-gather.2
  96.6 66.9 reduce-scatter.2
  214.5 32.6 all-gather.4
  251.9 67.0 reduce-scatter.4
where the time goes:
time: 328 us; the launch traced here: 327 us
  waiting for transfers between devices  209 us (64%)
  blocking collectives  56.6 us (17%)
  starting transfers between devices  20.3 us (6%)
  other arithmetic  14.3 us (4%)
  between operations  13.3 us (4%)
  matrix products  9.2 us (3%)
  local copies, waits for them, and re-layouts  4.19 us (1%)
    reduce_scatter x2, waiting for transfers between devices, one_block(): lax.psum_scatter(partial_value.astype(jnp.bfloat16), 'tensor', scatter_di...  134 us
    all_gather x2, waiting for transfers between devices, one_block(): lax.all_gather(normed_part, 'tensor', axis=1, tiled=True)  67.8 us
    psum x2, blocking collectives, one_block(): lax.psum((jnp.sum(filtered, axis=-1), jnp.sum(filtered * filtered, axis=-...  56.6 us
    ppermute x2, starting transfers between devices, with_halo(): after = lax.ppermute(leading, axis, down)  12.1 us
    dot_general x2, matrix products, one_block(): jnp.dot(hidden, reduce_w, preferred_element_type=jnp.float32)  9.2 us
    reduce_sum x2, other arithmetic, one_block(): jnp.sum(filtered, axis=-1)  9.17 us
    ppermute x2, starting transfers between devices, with_halo(): before = lax.ppermute(last, axis, up)  8 us
    ppermute x2, waiting for transfers between devices, with_halo(): before = lax.ppermute(last, axis, up)  7.13 us
  transfers between devices with their start and end apart: 8, of which 6 were waited for; matrix products, arithmetic and copies ran while one was open for 1% of the time, Pallas kernels for 0%

commit v1 on v0

--- a/solution.py
+++ b/solution.py
@@ -45,11 +45,14 @@
     normed_part = ((filtered - mean) / jnp.sqrt(var + 1e-06) * gain_part + bias_part).astype(
         jnp.bfloat16
     )
-    preact = jnp.dot(
-        lax.all_gather(normed_part, "tensor", axis=1, tiled=True),
-        expand,
-        preferred_element_type=jnp.float32,
-    )
+
+    def refer_columns_up(block_here):
+        left_arr = lax.all_to_all(
+            jnp.stack([block_here for _ in range(lax.axis_size("tensor"))]), "tensor", 0, 0
+        )
+        return jnp.concatenate(left_arr, axis=1)
+
+    preact = jnp.dot(refer_columns_up(normed_part), expand, preferred_element_type=jnp.float32)
     hidden = jax.nn.gelu(preact + bias_expand, approximate=False).astype(jnp.bfloat16)
     partial_value = jnp.dot(hidden, reduce_w, preferred_element_type=jnp.float32)
     mixed = lax.psum_scatter(

time: 328 us -> 290 us (0.88)
  waiting for transfers between devices: 209 us -> 150 us
  blocking collectives: 56.6 us -> 75.8 us
  starting transfers between devices: 20.3 us -> 24.2 us
    all_gather x2 -> x0, waiting for transfers between devices: 67.8 us -> none  [one_block(): lax.all_gather(normed_part, 'tensor', axis=1, tiled=True)]
    all_to_all x0 -> x1, blocking collectives: none -> 19.1 us  [refer_columns_up(): lax.all_to_all(jnp.stack([block_here for _ in range(lax.axis_size('tensor...]
    all_to_all x0 -> x1, waiting for transfers between devices: none -> 16.5 us  [refer_columns_up(): lax.all_to_all(jnp.stack([block_here for _ in range(lax.axis_size('tensor...]
    reduce_scatter x2, waiting for transfers between devices: 134 us -> 126 us  [one_block(): lax.psum_scatter(partial_value.astype(jnp.bfloat16), 'tensor', scatter_di...]
    all_to_all x0 -> x1, starting transfers between devices: none -> 3.78 us  [refer_columns_up(): lax.all_to_all(jnp.stack([block_here for _ in range(lax.axis_size('tensor...]
  transfers between devices with their start and end apart: 8 -> 7, of which waited for: 6 -> 5; matrix products, arithmetic and copies ran while one was open for 1% -> 1% of each run, Pallas kernels for 0% -> 0%
where the time goes in v1:
time: 290 us; the launch traced here: 289 us
  waiting for transfers between devices  150 us (52%)
  blocking collectives  75.8 us (26%)
  starting transfers between devices  24.2 us (8%)
  between operations  13.6 us (5%)
  other arithmetic  13 us (4%)
  matrix products  6.72 us (2%)
  local copies, waits for them, and re-layouts  5.36 us (2%)
    reduce_scatter x2, waiting for transfers between devices, one_block(): lax.psum_scatter(partial_value.astype(jnp.bfloat16), 'tensor', scatter_di...  126 us
    psum x2, blocking collectives, one_block(): lax.psum((jnp.sum(filtered, axis=-1), jnp.sum(filtered * filtered, axis=-...  56.7 us
    all_to_all x1, blocking collectives, refer_columns_up(): lax.all_to_all(jnp.stack([block_here for _ in range(lax.axis_size('tensor...  19.1 us
    all_to_all x1, waiting for transfers between devices, refer_columns_up(): lax.all_to_all(jnp.stack([block_here for _ in range(lax.axis_size('tensor...  16.5 us
    ppermute x2, starting transfers between devices, with_halo(): after = lax.ppermute(leading, axis, down)  12.3 us
    reduce_sum x2, other arithmetic, one_block(): jnp.sum(filtered, axis=-1)  9.19 us
    ppermute x2, starting transfers between devices, with_halo(): before = lax.ppermute(last, axis, up)  8 us
    ppermute x2, waiting for transfers between devices, with_halo(): before = lax.ppermute(last, axis, up)  7.19 us
  transfers between devices with their start and end apart: 7, of which 5 were waited for; matrix products, arithmetic and copies ran while one was open for 1% of the time, Pallas kernels for 0%

profile of v1, /device:TPU:8, one launch (start us, length us, event | category | flops | bytes accessed | tf_op | source)
XLA Modules:
  0.0 288.9 jit_solution(10442654575009390091)
XLA Ops:
  6.5 0.9 fusion.455
  7.4 6.1 %collective-permute-start = (bf16[3,128,64]{1,2,0:T(8,128)(2,1)S(1)}, bf16[3,128,64]{1,2,0:T(8,128)(2,1)S(1)}, u32[]{:S(2)}, u32[]{:S(2)}) collective-permute-start(bf16[3,128,64]{1,2,0:T(8,128)(2,1)S(1)} %get-tuple-element.17), channel_id=1, source_target_pairs={{0,16},{16,32},{32,48},{48,64},{64,80},{80,96},{96,112},{112,128},... | collective-permute-start | bytes 147464 | tf_op jit(solution)/shard_map/ppermute | solution.py:18
  13.5 6.7 %collective-permute-start.1 = (bf16[3,128,64]{1,2,0:T(8,128)(2,1)S(1)}, bf16[3,128,64]{1,2,0:T(8,128)(2,1)S(1)}, u32[]{:S(2)}, u32[]{:S(2)}) collective-permute-start(bf16[3,128,64]{1,2,0:T(8,128)(2,1)S(1)} %get-tuple-element.18), channel_id=1, source_target_pairs={{16,0},{32,16},{48,32},{64,48},{80,64},{96,80},{112,96},{128,112},... | collective-permute-start | bytes 147464 | tf_op jit(solution)/shard_map/ppermute | solution.py:19
  20.2 0.9 fusion.456
  21.1 0.8 fusion.457
  21.9 0.8 fusion.458
  23.3 0.9 maximum_convert_fusion.1
  24.2 2.2 fusion.451
  26.3 29.5 %all-reduce.3 = (f32[512]{0:T(512)S(1)}, f32[512]{0:T(512)S(1)}) all-reduce(f32[512]{0:T(512)S(1)} %bitcast.592, f32[512]{0:T(512)S(1)} %bitcast.591), channel_id=1, replica_groups=mesh['space'=32,'tensor'=16] {'tensor'}, use_global_device_ids=true, to_apply=%region_3.4 | all-reduce | flops 1024 | bytes 8192 | tf_op jit(solution)/shard_map/psum | solution.py:40
  56.0 1.1 stack.4
  57.1 3.8 %all-to-all-start = ((bf16[16,512,64]{1,2,0:T(8,128)(2,1)}), bf16[16,512,64]{1,2,0:T(8,128)(2,1)S(1)}, u32[]{:S(2)}, u32[]{:S(2)}) async-start(bf16[16,512,64]{1,2,0:T(8,128)(2,1)} %stack.4), calls=%async_computation | async-start | bytes 2097152 | tf_op jit(solution)/shard_map/all_to_all | solution.py:50
  60.9 16.5 %all-to-all-done = bf16[16,512,64]{1,2,0:T(8,128)(2,1)S(1)} async-done(((bf16[16,512,64]{1,2,0:T(8,128)(2,1)}), bf16[16,512,64]{1,2,0:T(8,128)(2,1)S(1)}, u32[]{:S(2)}, u32[]{:S(2)}) %all-to-all-start) | async-done | bytes 1048608 | tf_op jit(solution)/shard_map/all_to_all | solution.py:50
  77.4 3.4 %convolution_convert_fusion.1 = bf16[512,1024]{0,1:T(8,128)(2,1)} fusion(bf16[2,256,1024]{2,1,0:T(8,128)(2,1)S(1)} %copy-done.4, bf16[512,1024]{0,1:T(8,128)(2,1)S(1)} %bitcast.588, bf16[2,1024,256]{2,1,0:T(8,128)(2,1)S(1)} %copy-done.5, f32[256]{0:T(256)S(1)} %bitcast.596), kind=kOutput, calls=%fused_computation.85 | convolution fusion | flops 546045952 | bytes 3146752 | tf_op jit(solution)/shard_map/dot_general | solution.py:57
  81.5 63.9 %reduce-scatter.3.cloned.1.call-done = bf16[512,64]{0,1:T(8,128)(2,1)} async-done(((bf16[512,1024]{0,1:T(8,128)(2,1)}), bf16[512,64]{0,1:T(8,128)(2,1)}) %reduce-scatter.3.cloned.1.call-update) | async-done | bytes 65552 | tf_op jit(solution)/shard_map/reduce_scatter | solution.py:58
  145.4 0.9 fusion.284
  146.4 5.6 %collective-permute-start.3 = (bf16[3,128,64]{1,0,2:T(4,128)(2,1)S(1)}, bf16[3,128,64]{1,0,2:T(4,128)(2,1)S(1)}, u32[]{:S(2)}, u32[]{:S(2)}) collective-permute-start(bf16[3,128,64]{1,0,2:T(4,128)(2,1)S(1)} %slice.780), channel_id=1, source_target_pairs={{16,0},{32,16},{48,32},{64,48},{80,64},{96,80},{112,96},{128,112},... | collective-permute-start | bytes 147464 | tf_op jit(solution)/shard_map/ppermute | solution.py:19
  152.1 1.9 collective-permute-start.2
  154.1 7.2 %collective-permute-done.2 = bf16[3,128,64]{1,0,2:T(4,128)(2,1)S(1)} collective-permute-done((bf16[3,128,64]{1,0,2:T(4,128)(2,1)S(1)}, bf16[3,128,64]{1,0,2:T(4,128)(2,1)S(1)}, u32[]{:S(2)}, u32[]{:S(2)}) %collective-permute-start.2) | collective-permute-done | bytes 49184 | tf_op jit(solution)/shard_map/ppermute | solution.py:18
  161.4 7.0 %fusion.450 = (f32[4,128]{1,0:T(4,128)S(1)}, f32[4,128]{1,0:T(4,128)S(1)}, f32[4,128,64]{1,0,2:T(4,128)S(1)}) fusion(f32[64]{0:T(128)S(1)} %get-tuple-element.22, f32[64]{0:T(128)S(1)} %get-tuple-element.23, f32[64]{0:T(128)S(1)} %get-tuple-element.24, f32[64]{0:T(128)S(1)} %get-tuple-element.25, f32[10,128,64]{1,0,2:T(8,128)S(1)} %maximum_convert_fusion, ...), kind=kLoop, calls=%fused_computation.684 | loop fusion | flops 3275776 | bytes 1602048 | tf_op jit(solution)/shard_map/reduce_sum | solution.py:41
  168.4 27.1 %all-reduce.2 = (f32[512]{0:T(512)S(1)}, f32[512]{0:T(512)S(1)}) all-reduce(f32[512]{0:T(512)S(1)} %bitcast.594, f32[512]{0:T(512)S(1)} %bitcast.593), channel_id=1, replica_groups=mesh['space'=32,'tensor'=16] {'tensor'}, use_global_device_ids=true, to_apply=%region_8.9 | all-reduce | flops 1024 | bytes 8192 | tf_op jit(solution)/shard_map/psum | solution.py:40
  195.8 19.1 %all_to_all.10 = bf16[16,512,64]{1,2,0:T(8,128)(2,1)S(1)} all-to-all(bf16[16,512,64]{1,2,0:T(8,128)(2,1)S(1)} %stack.5), channel_id=1, replica_groups=mesh['space'=32,'tensor'=16] {'tensor'}, dimensions={0} | all-to-all | bytes 2097152 | tf_op jit(solution)/shard_map/all_to_all | solution.py:50
  214.9 3.4 %convolution_convert_fusion = bf16[512,1024]{0,1:T(8,128)(2,1)} fusion(bf16[2,256,1024]{2,1,0:T(8,128)(2,1)S(1)} %copy-done.4, bf16[512,1024]{0,1:T(8,128)(2,1)S(1)} %bitcast.589, bf16[2,1024,256]{2,1,0:T(8,128)(2,1)S(1)} %copy-done.5, f32[256]{0:T(256)S(1)} %bitcast.595), kind=kOutput, calls=%fused_computation.84 | convolution fusion | flops 546045952 | bytes 3146752 | tf_op jit(solution)/shard_map/dot_general | solution.py:57
  218.3 62.2 %reduce-scatter.5.cloned.1.call-done = bf16[512,64]{0,1:T(8,128)(2,1)} async-done(((bf16[512,1024]{0,1:T(8,128)(2,1)}), bf16[512,64]{0,1:T(8,128)(2,1)}) %reduce-scatter.5.cloned.1.call-update) | async-done | bytes 65552 | tf_op jit(solution)/shard_map/reduce_scatter | solution.py:58
  280.5 1.6 copy_bitcast_fusion
  (40 shorter events, 2.0 us)
Async XLA Ops:
  7.4 15.4 %collective-permute-start = (bf16[3,128,64]{1,2,0:T(8,128)(2,1)S(1)}, bf16[3,128,64]{1,2,0:T(8,128)(2,1)S(1)}, u32[]{:S(2)}, u32[]{:S(2)}) collective-permute-start(bf16[3,128,64]{1,2,0:T(8,128)(2,1)S(1)} %get-tuple-element.17), channel_id=1, source_target_pairs={{0,16},{16,32},{32,48},{48,64},{64,80},{80,96},{96,112},{112,128},... | collective-permute-start | bytes 147464 | tf_op jit(solution)/shard_map/ppermute | solution.py:18
  13.5 9.8 %collective-permute-start.1 = (bf16[3,128,64]{1,2,0:T(8,128)(2,1)S(1)}, bf16[3,128,64]{1,2,0:T(8,128)(2,1)S(1)}, u32[]{:S(2)}, u32[]{:S(2)}) collective-permute-start(bf16[3,128,64]{1,2,0:T(8,128)(2,1)S(1)} %get-tuple-element.18), channel_id=1, source_target_pairs={{16,0},{32,16},{48,32},{64,48},{80,64},{96,80},{112,96},{128,112},... | collective-permute-start | bytes 147464 | tf_op jit(solution)/shard_map/ppermute | solution.py:19
  57.0 3.8 %copy-start.1 = (f32[2,256]{1,0:T(2,128)S(1)}, f32[2,256]{1,0:T(2,128)}, u32[]{:S(2)}) copy-start(f32[2,256]{1,0:T(2,128)} %param.14) | copy-start | bytes 6148
  57.0 20.4 %copy-start.4 = (bf16[2,256,1024]{2,1,0:T(8,128)(2,1)S(1)}, bf16[2,256,1024]{2,1,0:T(8,128)(2,1)}, u32[]{:S(2)}) copy-start(bf16[2,256,1024]{2,1,0:T(8,128)(2,1)} %param.15) | copy-start | bytes 3145732
  57.0 20.4 %copy-start.5 = (bf16[2,1024,256]{2,1,0:T(8,128)(2,1)S(1)}, bf16[2,1024,256]{2,1,0:T(8,128)(2,1)}, u32[]{:S(2)}) copy-start(bf16[2,1024,256]{2,1,0:T(8,128)(2,1)} %param.13) | copy-start | bytes 3145732
  57.1 20.4 %all-to-all-start = ((bf16[16,512,64]{1,2,0:T(8,128)(2,1)}), bf16[16,512,64]{1,2,0:T(8,128)(2,1)S(1)}, u32[]{:S(2)}, u32[]{:S(2)}) async-start(bf16[16,512,64]{1,2,0:T(8,128)(2,1)} %stack.4), calls=%async_computation | async-start | bytes 2097152 | tf_op jit(solution)/shard_map/all_to_all | solution.py:50
  60.8 84.6 %reduce-scatter.3.cloned.1.call-start = ((), (), s32[]{:S(2)}) async-start(), calls=%async_computation.4 | async-start | bytes 1114112 | tf_op jit(solution)/shard_map/reduce_scatter | solution.py:58
  80.8 0.7 copy-start.2
  80.8 0.7 copy-start.3
  80.8 64.6 %copy-start = (bf16[4,128,64]{1,2,0:T(8,128)(2,1)S(1)}, bf16[4,128,64]{1,2,0:T(8,128)(2,1)}, u32[]{:S(2)}) copy-start(bf16[4,128,64]{1,2,0:T(8,128)(2,1)} %param.9) | copy-start | bytes 196612
  80.8 199.7 %reduce-scatter.5.cloned.1.call-start = ((), (), s32[]{:S(2)}) async-start(), calls=%async_computation.5 | async-start | bytes 1114112 | tf_op jit(solution)/shard_map/reduce_scatter | solution.py:58
  146.4 7.6 %collective-permute-start.3 = (bf16[3,128,64]{1,0,2:T(4,128)(2,1)S(1)}, bf16[3,128,64]{1,0,2:T(4,128)(2,1)S(1)}, u32[]{:S(2)}, u32[]{:S(2)}) collective-permute-start(bf16[3,128,64]{1,0,2:T(4,128)(2,1)S(1)} %slice.780), channel_id=1, source_target_pairs={{16,0},{32,16},{48,32},{64,48},{80,64},{96,80},{112,96},{128,112},... | collective-permute-start | bytes 147464 | tf_op jit(solution)/shard_map/ppermute | solution.py:19
  152.1 9.2 %collective-permute-start.2 = (bf16[3,128,64]{1,0,2:T(4,128)(2,1)S(1)}, bf16[3,128,64]{1,0,2:T(4,128)(2,1)S(1)}, u32[]{:S(2)}, u32[]{:S(2)}) collective-permute-start(bf16[3,128,64]{1,0,2:T(4,128)(2,1)S(1)} %slice.778), channel_id=1, source_target_pairs={{0,16},{16,32},{32,48},{48,64},{64,80},{80,96},{96,112},{112,128},... | collective-permute-start | bytes 147464 | tf_op jit(solution)/shard_map/ppermute | solution.py:18
Sparse Core Ops, SparseCore 0:
  80.9 64.4 reduce-scatter.2
  218.4 62.0 reduce-scatter.4
